TPU v7x, 32 devices: a whole 2x2x4 slice. The times are simulated.
32 devices in a mesh: req: 4 (over y, core), seq: 8 (over z, x).
Axes of the slice: x: 2, y: 2, z: 4, core: 2. Of those that a mesh axis runs over, the one named last changes fastest.
Arguments:
- embedded: bfloat16 [4, 48, 3584], P(None, 'req'), may hold values from -6 to 6
- cache_keys: bfloat16 [4, 4096, 2048], P('req', 'seq'), may hold values from -6 to 6
- cache_values: bfloat16 [4, 4096, 2048], P('req', 'seq'), may hold values from -6 to 6
- token_owner: int32 [4, 4096], P('req', 'seq'), may hold values from 0 to 11, as said below
- dealing: int32 [48], replicated, may hold values from 0 to 47, as said below
- lengths: int32 [48], replicated, may hold values from 1 to 2048, as said below
- project_weight: bfloat16 [3584, 8192], P(None, 'seq')
- output_weight: bfloat16 [4096, 3584], P('seq'), may hold values from -0.09375 to 0.09375
- gate_weight: bfloat16 [3584, 14336], P(None, ('req', 'seq')), may hold values from -0.09375 to 0.09375
- up_weight: bfloat16 [3584, 14336], P(None, ('req', 'seq')), may hold values from -0.09375 to 0.09375
- down_weight: bfloat16 [14336, 3584], P(('req', 'seq')), may hold values from -0.046875 to 0.046875
- gain_first: float32 [3584], replicated, may hold values from 0.1 to 1.9
- gain_second: float32 [3584], replicated, may hold values from 0.1 to 1.9
- gain_third: float32 [3584], replicated, may hold values from 0.1 to 1.9
- gain_fourth: float32 [3584], replicated, may hold values from 0.1 to 1.9
Outputs:
- results: bfloat16 [4, 48, 3584], P(None, 'req')
Inputs may be any that keep to these rules, and one draw needn't show every extreme that they name: A permutation of the requests; slot i of req group g serves request dealing[g * 12 + i]. The lengths of the 12 requests dealt to one group sum to 4096; in every group the longest is exactly 2048. `token_owner`: each slot owns a contiguous run of its group's pool, runs in slot order, as many tokens as its request's length.
All inputs are finite; a program needn't handle non-finite values.
Results may differ from a plain program's by a relative error of at most 0.012.
The roundings to bfloat16 on the way count: a program that leaves them out, or rounds other values in their place, can miss the bound.
Values may be sent and summed in bfloat16 or wider, within the bound.
A program may use at most 128 MiB of HBM per device.

v0:
```python
import math
import jax
import jax.numpy as jnp
from jax import lax
from jax.sharding import PartitionSpec as P

H = 16
KVH = 8
HD = 256
STEPS = 4
soft_cap = 50.0
epsilon = 1e-06


def rms_scale(values, gain):
    mean_square = jnp.mean(values * values, axis=-1, keepdims=True)
    return values * lax.rsqrt(mean_square + epsilon) * gain


def rotate(values, positions):
    half_width = values.shape[-1] // 2
    freq_index = jnp.arange(half_width, dtype=jnp.float32)
    inverse = jnp.exp(freq_index * (-2.0 * math.log(10000.0) / values.shape[-1]))
    angles = positions[:, None] * inverse[None, :]
    cosine = jnp.cos(angles)[:, None, :]
    sine = jnp.sin(angles)[:, None, :]
    first_half = values[..., :half_width]
    second_half = values[..., half_width:]
    return jnp.concatenate(
        [first_half * cosine - second_half * sine, second_half * cosine + first_half * sine],
        axis=-1,
    )


def capped_weight(scores):
    return jnp.exp(soft_cap * jnp.tanh(scores / soft_cap))


def rounded(values):
    return lax.optimization_barrier(values.astype(jnp.bfloat16)).astype(jnp.float32)


def body(
    embedded,
    cache_keys,
    cache_values,
    token_owner,
    dealing,
    lengths,
    project_weight,
    output_weight,
    gate_weight,
    up_weight,
    down_weight,
    gain_first,
    gain_second,
    gain_third,
    gain_fourth,
):
    row_count = embedded.shape[1]
    rows = STEPS * row_count
    width = embedded.shape[2]
    local_tokens = cache_keys.shape[1]
    value_width = cache_keys.shape[2]
    group_size = H // KVH
    attention_width = H * HD
    column_count = output_weight.shape[0]
    group_index = lax.axis_index("req")
    seq_index = lax.axis_index("seq")
    seq_size = lax.axis_size("seq")
    req_size = lax.axis_size("req")
    column_start = seq_index * column_count
    slot_requests = lax.dynamic_slice_in_dim(dealing, group_index * row_count, row_count)
    matches = slot_requests[:, None] == jnp.arange(dealing.shape[0], dtype=jnp.int32)[None, :]
    base_positions = jnp.sum(jnp.where(matches, lengths[None, :], 0), axis=1)
    positions = base_positions[None, :] + jnp.arange(STEPS, dtype=jnp.int32)[:, None]
    positions = positions.reshape(rows).astype(jnp.float32)
    key_pool = cache_keys[0].reshape(local_tokens, KVH, HD)
    value_pool = cache_values[0].reshape(local_tokens, KVH, HD)
    slots = jnp.tile(jnp.arange(row_count, dtype=jnp.int32), STEPS)
    moments = jnp.repeat(jnp.arange(STEPS, dtype=jnp.int32), row_count)
    owned_mask = token_owner[0][None, :] == slots[:, None]
    stream = embedded.reshape(rows, width).astype(jnp.float32)
    normed = rms_scale(stream, gain_first).astype(jnp.bfloat16)
    local_part = jnp.dot(normed, project_weight, preferred_element_type=jnp.float32).astype(
        jnp.bfloat16
    )
    projected = lax.all_gather(local_part, "seq", axis=1, tiled=True)
    query_rows = projected[:, :attention_width].astype(jnp.float32).reshape(rows, H, HD)
    queries = (rotate(query_rows, positions) * HD ** (-0.5)).astype(jnp.bfloat16)
    key_rows = (
        projected[:, attention_width : attention_width + value_width]
        .astype(jnp.float32)
        .reshape(rows, KVH, HD)
    )
    fresh_keys = rotate(key_rows, positions).astype(jnp.bfloat16)
    fresh_values = projected[:, attention_width + value_width :].reshape(rows, KVH, HD)
    grouped = queries.reshape(rows, KVH, group_size, HD)
    all_keys = jnp.concatenate([key_pool, fresh_keys], axis=0)
    all_values = jnp.concatenate([value_pool, fresh_values], axis=0)
    fresh_mask = (
        (slots[None, :] == slots[:, None])
        & (moments[None, :] <= moments[:, None])
        & (seq_index == 0)
    )
    mask = jnp.concatenate([owned_mask, fresh_mask], axis=1)
    scores = jnp.einsum("igqd,tgd->igqt", grouped, all_keys, preferred_element_type=jnp.float32)
    weights = jnp.where(mask[:, None, None, :], capped_weight(scores), 0.0)
    totals = lax.psum(jnp.sum(weights, axis=-1), "seq").reshape(rows, H)
    outputs = jnp.einsum(
        "igqt,tgd->igqd",
        weights.astype(jnp.bfloat16),
        all_values,
        preferred_element_type=jnp.float32,
    ).reshape(rows, attention_width)
    outputs = lax.psum_scatter(outputs, "seq", scatter_dimension=1, tiled=True)
    spread = jnp.repeat(totals, HD, axis=1)
    spread = lax.dynamic_slice_in_dim(spread, column_start, column_count, 1)
    attended = (outputs / spread).astype(jnp.bfloat16)
    partial = jnp.dot(attended, output_weight, preferred_element_type=jnp.float32)
    mixed = lax.psum(partial, "seq")
    middle = stream + rms_scale(mixed, gain_second)
    feed_input = rms_scale(middle, gain_third).astype(jnp.bfloat16)
    block_rows = lax.all_gather(feed_input, "req", axis=0, tiled=True)
    gate_part = jnp.dot(block_rows, gate_weight, preferred_element_type=jnp.float32)
    up_part = jnp.dot(block_rows, up_weight, preferred_element_type=jnp.float32)
    hidden = (jax.nn.gelu(gate_part, approximate=True) * up_part).astype(jnp.bfloat16)
    summed = jnp.dot(hidden, down_weight, preferred_element_type=jnp.float32)
    summed = lax.psum_scatter(summed, "req", scatter_dimension=0, tiled=True)
    summed = lax.psum(summed, "seq")
    results = (middle + rms_scale(summed, gain_fourth)).astype(jnp.bfloat16)
    return results.reshape(STEPS, row_count, width)


def solution(mesh):
    return jax.shard_map(
        body,
        mesh=mesh,
        in_specs=(
            P(None, "req", None),
            P("req", "seq", None),
            P("req", "seq", None),
            P("req", "seq"),
            P(),
            P(),
            P(None, "seq"),
            P("seq", None),
            P(None, ("req", "seq")),
            P(None, ("req", "seq")),
            P(("req", "seq"), None),
            P(),
            P(),
            P(),
            P(),
        ),
        out_specs=P(None, "req", None),
        check_vma=False,
    )
```

profile of v0, /device:TPU:0, one launch (start us, length us, event | category | flops | bytes accessed | tf_op | source)
XLA Modules:
  0.0 383.3 jit_solution(17114336762805842567)
XLA Ops:
  6.6 2.1 copy.64
  8.7 1.2 multiply_reduce_fusion.3
  9.9 2.1 reshape.160
  12.1 0.1 copy.86
  12.2 0.1 rsqrt.36
  12.2 4.8 %convolution_convert_fusion = bf16[48,1024]{1,0:T(8,128)(2,1)S(1)} fusion(bf16[3584,1024]{1,0:T(8,128)(2,1)} %param.21, f32[48,3584]{1,0:T(8,128)} %reshape.160, f32[3584]{0:T(1024)S(1)} %copy-done.4, f32[48]{0:T(128)S(1)} %rsqrt.36), kind=kOutput, calls=%fused_computation.14 | convolution fusion | flops 352886784 | bytes 8140992 | tf_op jit(solution)/shard_map/dot_general | solution.py:85
  17.0 0.0 copy-start.8
  17.0 0.0 copy-start.9
  17.0 33.8 %all_gather.6 = bf16[48,8192]{1,0:T(8,128)(2,1)S(1)} all-gather(bf16[48,1024]{1,0:T(8,128)(2,1)S(1)} %convolution_convert_fusion), channel_id=1, replica_groups=mesh['req'=4,'seq'=8] {'seq'}, dimensions={1}, use_global_device_ids=true | all-gather | bytes 884736 | tf_op jit(solution)/shard_map/all_gather | solution.py:88
  50.9 0.9 slice_convert_fusion.1
  51.7 0.9 slice_convert_fusion
  52.6 0.1 dynamic_slice.6
  52.7 0.2 select_reduce_fusion
  52.9 0.1 add.91
  53.0 0.1 le.17
  53.1 1.1 copy.83
  54.2 0.7 fusion.39
  54.9 1.4 copy.84
  56.3 0.2 multiply_cosine_fusion
  56.5 0.1 multiply_subtract_fusion
  56.6 0.9 copy.73
  57.5 0.9 copy.74
  58.3 0.1 eq.50
  58.4 0.1 and_and_fusion
  58.5 0.1 broadcast_compare_fusion
  58.6 3.9 %copy.69 = bf16[1,512,2048]{1,2,0:T(8,128)(2,1)} copy(bf16[1,512,2048]{2,1,0:T(8,128)(2,1)} %param.16) | data formatting | bytes 4194304 | tf_op args[1]
  62.6 3.9 %copy.72 = bf16[512,8,256]{2,0,1:T(8,128)(2,1)} copy(bf16[512,8,256]{0,2,1:T(8,128)(2,1)} %bitcast.44) | data formatting | bytes 4194304 | tf_op jit(solution)/shard_map/reshape;squeeze | solution.py:78
  66.5 1.6 copy.92
  68.1 3.9 %copy.65 = bf16[1,512,2048]{1,2,0:T(8,128)(2,1)} copy(bf16[1,512,2048]{2,1,0:T(8,128)(2,1)} %param.17) | data formatting | bytes 4194304 | tf_op args[2]
  72.0 3.9 %copy.67 = bf16[512,8,256]{2,0,1:T(8,128)(2,1)} copy(bf16[512,8,256]{0,2,1:T(8,128)(2,1)} %bitcast.45) | data formatting | bytes 4194304 | tf_op jit(solution)/shard_map/reshape;squeeze | solution.py:79
  76.0 1.0 subtract_convert_fusion
  77.0 2.9 fusion.40
  80.0 0.6 fusion.8
  80.5 1.5 copy.75
  82.1 2.6 reshape.156
  84.7 0.0 reduce-scatter.3.cloned.1.call-update
  84.7 0.0 all-reduce.3.cloned.1.call-start
  84.8 21.7 %psum.21 = f32[48,16]{0,1:T(8,128)S(1)} all-reduce(f32[48,16]{0,1:T(8,128)S(1)} %bitcast.56), channel_id=1, replica_groups=mesh['req'=4,'seq'=8] {'seq'}, use_global_device_ids=true, to_apply=%region_4.5 | all-reduce | flops 768 | bytes 6144 | tf_op jit(solution)/shard_map/psum | solution.py:109
  106.4 0.1 copy.76
  106.5 0.2 broadcast_in_dim.35
  106.7 1.4 copy.85
  108.1 40.9 %reduce-scatter.3.cloned.1.call-done = f32[48,512]{1,0:T(8,128)} async-done(((f32[48,4096]{1,0:T(8,128)}), f32[48,512]{1,0:T(8,128)}) %reduce-scatter.3.cloned.1.call-update) | async-done | bytes 98320 | tf_op jit(solution)/shard_map/reduce_scatter | solution.py:116
  149.0 3.8 fusion.29
  152.7 0.0 all-reduce.3.cloned.1.call-update
  152.7 0.0 all-gather.2.cloned.1.call-start
  152.8 72.8 %all-reduce.3.cloned.1.call-done = f32[48,3584]{1,0:T(8,128)} async-done(((f32[48,3584]{1,0:T(8,128)}), f32[48,3584]{1,0:T(8,128)}) %all-reduce.3.cloned.1.call-update) | async-done | bytes 688144 | tf_op jit(solution)/shard_map/psum | solution.py:121
  225.6 1.2 multiply_reduce_fusion.2
  226.9 1.6 multiply_reduce_fusion.1
  228.5 0.8 copy-done.1
  229.3 0.9 multiply_convert_fusion
  230.2 0.0 all-gather.2.cloned.1.call-update
  230.2 0.0 reduce-scatter.5.cloned.1.call-start
  230.3 17.7 %all-gather.2.cloned.1.call-done = bf16[192,3584]{1,0:T(8,128)(2,1)} async-done(((bf16[48,3584]{1,0:T(8,128)(2,1)}), bf16[192,3584]{1,0:T(8,128)(2,1)}) %all-gather.2.cloned.1.call-update) | async-done | bytes 1376272 | tf_op jit(solution)/shard_map/all_gather | solution.py:124
  247.9 4.1 %fusion.41 = f32[192,448]{1,0:T(8,128)} fusion(bf16[192,3584]{1,0:T(8,128)(2,1)} %all-gather.2.cloned.1.call-done, bf16[3584,448]{0,1:T(8,128)(2,1)} %param.23), kind=kOutput, calls=%fused_computation.75 | convolution fusion | flops 616562688 | bytes 4931584 | tf_op jit(solution)/shard_map/dot_general | solution.py:125
  252.1 6.0 %fusion.10 = f32[192,3584]{1,0:T(8,128)} fusion(bf16[448,3584]{1,0:T(8,128)(2,1)S(1)} %copy-done, bf16[192,3584]{1,0:T(8,128)(2,1)} %all-gather.2.cloned.1.call-done, bf16[3584,448]{0,1:T(8,128)(2,1)} %param.24, f32[192,448]{1,0:T(8,128)} %fusion.41), kind=kOutput, calls=%fused_computation.15 | convolution fusion | flops 1233985536 | bytes 10895360 | tf_op jit(solution)/shard_map/dot_general | solution.py:128
  258.1 0.0 reduce-scatter.5.cloned.1.call-update
  258.1 0.0 all-reduce.5.cloned.1.call-start
  258.2 35.6 %reduce-scatter.5.cloned.1.call-done = f32[48,3584]{1,0:T(8,128)} async-done(((f32[192,3584]{1,0:T(8,128)}), f32[48,3584]{1,0:T(8,128)}) %reduce-scatter.5.cloned.1.call-update) | async-done | bytes 688144 | tf_op jit(solution)/shard_map/reduce_scatter | solution.py:129
  293.7 0.0 all-reduce.5.cloned.1.call-update
  293.8 77.4 %all-reduce.5.cloned.1.call-done = f32[48,3584]{1,0:T(8,128)} async-done(((f32[48,3584]{1,0:T(8,128)}), f32[48,3584]{1,0:T(8,128)}) %all-reduce.5.cloned.1.call-update) | async-done | bytes 688144 | tf_op jit(solution)/shard_map/psum | solution.py:130
  371.1 1.2 multiply_reduce_fusion
  372.4 1.5 add_convert_fusion
  373.9 0.9 reshape.159
  374.7 2.0 copy.77
  (28 shorter events, 0.1 us)
Async XLA Ops:
  6.5 245.5 %copy-start = (bf16[448,3584]{1,0:T(8,128)(2,1)S(1)}, bf16[448,3584]{1,0:T(8,128)(2,1)}, u32[]{:S(2)}) copy-start(bf16[448,3584]{1,0:T(8,128)(2,1)} %param.25) | copy-start | bytes 9633796
  6.5 5.7 %copy-start.4 = (f32[3584]{0:T(1024)S(1)}, f32[3584]{0:T(1024)}, u32[]{:S(2)}) copy-start(f32[3584]{0:T(1024)} %param.26) | copy-start | bytes 43012
  6.5 142.4 %reduce-scatter.3.cloned.1.call-start = ((), (), s32[]{:S(2)}) async-start(), calls=%async_computation.2 | async-start | bytes 884736 | tf_op jit(solution)/shard_map/reduce_scatter | solution.py:116
  17.0 35.6 %copy-start.8 = (s32[48]{0:T(128)S(1)}, s32[48]{0:T(128)}, u32[]{:S(2)}) copy-start(s32[48]{0:T(128)} %param.19) | copy-start | bytes 580
  17.0 35.7 %copy-start.9 = (s32[48]{0:T(128)S(1)}, s32[48]{0:T(128)}, u32[]{:S(2)}) copy-start(s32[48]{0:T(128)} %param.20) | copy-start | bytes 580
  54.9 3.6 copy-start.7
  77.0 2.9 copy-start.2
  77.0 2.9 copy-start.3
  84.7 140.9 %all-reduce.3.cloned.1.call-start = ((), (), s32[]{:S(2)}) async-start(), calls=%async_computation.3 | async-start | bytes 1376256 | tf_op jit(solution)/shard_map/psum | solution.py:121
  149.0 77.9 %copy-start.6 = (f32[3584]{0:T(1024)S(1)}, f32[3584]{0:T(1024)}, u32[]{:S(2)}) copy-start(f32[3584]{0:T(1024)} %param.27) | copy-start | bytes 43012
  152.7 76.6 %copy-start.5 = (f32[3584]{0:T(1024)S(1)}, f32[3584]{0:T(1024)}, u32[]{:S(2)}) copy-start(f32[3584]{0:T(1024)} %param.28) | copy-start | bytes 43012
  152.7 95.2 %all-gather.2.cloned.1.call-start = ((), (), s32[]{:S(2)}) async-start(), calls=%async_computation.4 | async-start | bytes 1720320 | tf_op jit(solution)/shard_map/all_gather | solution.py:124
  228.4 0.9 copy-start.1
  230.2 63.5 %reduce-scatter.5.cloned.1.call-start = ((), (), s32[]{:S(2)}) async-start(), calls=%async_computation.5 | async-start | bytes 3440640 | tf_op jit(solution)/shard_map/reduce_scatter | solution.py:129
  258.1 113.0 %all-reduce.5.cloned.1.call-start = ((), (), s32[]{:S(2)}) async-start(), calls=%async_computation.6 | async-start | bytes 1376256 | tf_op jit(solution)/shard_map/psum | solution.py:130
Sparse Core Ops, SparseCore 0:
  84.8 64.0 reduce-scatter.2
  152.9 72.6 all-reduce.2
  230.3 17.5 all-gather.1
  258.2 35.4 reduce-scatter.4
  297.4 73.6 all-reduce.4
where the time goes:
time: 384 us; the launch traced here: 383 us
  waiting for transfers between devices  244 us (64%)
  blocking collectives  55.5 us (14%)
  local copies, waits for them, and re-layouts  36.6 us (10%)
  matrix products  22.2 us (6%)
  between operations  13.3 us (3%)
  other arithmetic  11.1 us (3%)
    psum x1, waiting for transfers between devices, body(): summed = lax.psum(summed, 'seq')  77.4 us
    psum x1, waiting for transfers between devices, body(): mixed = lax.psum(partial, 'seq')  72.8 us
    reduce_scatter x1, waiting for transfers between devices, body(): outputs = lax.psum_scatter(outputs, 'seq', scatter_dimension=1, tiled=True)  40.9 us
    reduce_scatter x1, waiting for transfers between devices, body(): summed = lax.psum_scatter(summed, 'req', scatter_dimension=0, tiled=True)  35.6 us
    all_gather x1, blocking collectives, body(): projected = lax.all_gather(local_part, 'seq', axis=1, tiled=True)  33.8 us
    psum x1, blocking collectives, body(): totals = lax.psum(jnp.sum(weights, axis=-1), 'seq').reshape(rows, H)  21.7 us
    all_gather x1, waiting for transfers between devices, body(): block_rows = lax.all_gather(feed_input, 'req', axis=0, tiled=True)  17.7 us
    unnamed x26, local copies, waits for them, and re-layouts  12.7 us
  transfers between devices with their start and end apart: 5, of which 5 were waited for; matrix products, arithmetic and copies ran while one was open for 0% of the time, Pallas kernels for 0%

commit v1 on v0

--- a/solution.py
+++ b/solution.py
@@ -121,7 +121,12 @@
     mixed = lax.psum(partial, "seq")
     middle = stream + rms_scale(mixed, gain_second)
     feed_input = rms_scale(middle, gain_third).astype(jnp.bfloat16)
-    block_rows = lax.all_gather(feed_input, "req", axis=0, tiled=True)
+    ring = [feed_input]
+    for hop in range(3):
+        ring.append(lax.ppermute(ring[-1], "req", [(dev, (dev + 1) % 4) for dev in range(4)]))
+    block_rows = jnp.roll(
+        jnp.concatenate(ring[::-1], axis=0), (lax.axis_index("req") + 1) * ring[0].shape[0], axis=0
+    )
     gate_part = jnp.dot(block_rows, gate_weight, preferred_element_type=jnp.float32)
     up_part = jnp.dot(block_rows, up_weight, preferred_element_type=jnp.float32)
     hidden = (jax.nn.gelu(gate_part, approximate=True) * up_part).astype(jnp.bfloat16)

time: 384 us -> 389 us (1.013)
  local copies, waits for them, and re-layouts: 36.6 us -> 41.2 us
    ppermute x0 -> x3, waiting for transfers between devices: none -> 20.4 us  [body(): lax.ppermute(ring[-1], 'req', [(dev, (dev + 1) % 4) for dev in range(4)])]
    all_gather x1 -> x0, waiting for transfers between devices: 17.7 us -> none  [body(): block_rows = lax.all_gather(feed_input, 'req', axis=0, tiled=True)]
    unnamed x26 -> x44, local copies, waits for them, and re-layouts: 12.7 us -> 18.5 us
  transfers between devices with their start and end apart: 5 -> 7, of which waited for: 5 -> 7; matrix products, arithmetic and copies ran while one was open for 0% -> 0% of each run, Pallas kernels for 0% -> 0%
where the time goes in v1:
time: 389 us; the launch traced here: 388 us
  waiting for transfers between devices  246 us (63%)
  blocking collectives  55.6 us (14%)
  local copies, waits for them, and re-layouts  41.2 us (11%)
  matrix products  19.9 us (5%)
  between operations  13.4 us (3%)
  other arithmetic  11.9 us (3%)
    psum x1, waiting for transfers between devices, body(): summed = lax.psum(summed, 'seq')  77.4 us
    psum x1, waiting for transfers between devices, body(): mixed = lax.psum(partial, 'seq')  72.8 us
    reduce_scatter x1, waiting for transfers between devices, body(): outputs = lax.psum_scatter(outputs, 'seq', scatter_dimension=1, tiled=True)  40.9 us
    reduce_scatter x1, waiting for transfers between devices, body(): summed = lax.psum_scatter(summed, 'req', scatter_dimension=0, tiled=True)  34.6 us
    all_gather x1, blocking collectives, body(): projected = lax.all_gather(local_part, 'seq', axis=1, tiled=True)  33.9 us
    psum x1, blocking collectives, body(): totals = lax.psum(jnp.sum(weights, axis=-1), 'seq').reshape(rows, H)  21.7 us
    ppermute x3, waiting for transfers between devices, body(): lax.ppermute(ring[-1], 'req', [(dev, (dev + 1) % 4) for dev in range(4)])  20.4 us
    unnamed x44, local copies, waits for them, and re-layouts  18.5 us
  transfers between devices with their start and end apart: 7, of which 7 were waited for; matrix products, arithmetic and copies ran while one was open for 0% of the time, Pallas kernels for 0%

profile of v1, /device:TPU:0, one launch (start us, length us, event | category | flops | bytes accessed | tf_op | source)
XLA Modules:
  0.0 388.4 jit_solution(3359949737988268971)
XLA Ops:
  6.6 1.4 multiply_reduce_fusion.3
  7.9 2.0 copy.64
  9.9 0.1 copy.86
  10.0 0.1 rsqrt.36
  10.1 2.1 reshape.160
  12.3 4.8 %convolution_convert_fusion = bf16[48,1024]{1,0:T(8,128)(2,1)S(1)} fusion(bf16[3584,1024]{1,0:T(8,128)(2,1)} %param.21, f32[48,3584]{1,0:T(8,128)} %reshape.160, f32[3584]{0:T(1024)S(1)} %copy-done.8, f32[48]{0:T(128)S(1)} %rsqrt.36), kind=kOutput, calls=%fused_computation.16 | convolution fusion | flops 352886784 | bytes 8140992 | tf_op jit(solution)/shard_map/dot_general | solution.py:85
  17.1 33.9 %all_gather.3 = bf16[48,8192]{1,0:T(8,128)(2,1)S(1)} all-gather(bf16[48,1024]{1,0:T(8,128)(2,1)S(1)} %convolution_convert_fusion), channel_id=1, replica_groups=mesh['req'=4,'seq'=8] {'seq'}, dimensions={1}, use_global_device_ids=true | all-gather | bytes 884736 | tf_op jit(solution)/shard_map/all_gather | solution.py:88
  51.0 0.8 slice_convert_fusion.1
  51.8 0.9 slice_convert_fusion
  52.7 0.1 dynamic_slice.10
  52.8 0.2 select_reduce_fusion
  53.0 0.1 add.104
  53.1 0.1 le.17
  53.2 0.1 eq.53
  53.3 0.1 and_and_fusion
  53.4 0.1 broadcast_compare_fusion
  53.5 1.4 copy.84
  54.9 1.1 copy.83
  56.0 0.7 copy.92
  56.7 0.7 fusion.54
  57.4 0.2 multiply_cosine_fusion
  57.5 0.1 multiply_subtract_fusion
  57.6 0.9 copy.73
  58.5 0.9 copy.74
  59.4 3.9 %copy.69 = bf16[1,512,2048]{1,2,0:T(8,128)(2,1)} copy(bf16[1,512,2048]{2,1,0:T(8,128)(2,1)} %param.16) | data formatting | bytes 4194304 | tf_op args[1]
  63.3 3.9 %copy.72 = bf16[512,8,256]{2,0,1:T(8,128)(2,1)} copy(bf16[512,8,256]{0,2,1:T(8,128)(2,1)} %bitcast.42) | data formatting | bytes 4194304 | tf_op jit(solution)/shard_map/reshape;squeeze | solution.py:78
  67.2 3.9 %copy.65 = bf16[1,512,2048]{1,2,0:T(8,128)(2,1)} copy(bf16[1,512,2048]{2,1,0:T(8,128)(2,1)} %param.17) | data formatting | bytes 4194304 | tf_op args[2]
  71.1 3.9 %copy.67 = bf16[512,8,256]{2,0,1:T(8,128)(2,1)} copy(bf16[512,8,256]{0,2,1:T(8,128)(2,1)} %bitcast.43) | data formatting | bytes 4194304 | tf_op jit(solution)/shard_map/reshape;squeeze | solution.py:79
  75.0 1.0 subtract_convert_fusion
  76.1 2.9 fusion.55
  79.0 0.6 fusion.8
  79.6 1.5 copy.75
  81.1 2.7 reshape.156
  83.8 0.0 all-reduce.3.cloned.1.call-start
  83.8 21.7 %psum.21 = f32[48,16]{0,1:T(8,128)S(1)} all-reduce(f32[48,16]{0,1:T(8,128)S(1)} %bitcast.54), channel_id=1, replica_groups=mesh['req'=4,'seq'=8] {'seq'}, use_global_device_ids=true, to_apply=%region_4.5 | all-reduce | flops 768 | bytes 6144 | tf_op jit(solution)/shard_map/psum | solution.py:109
  105.5 0.1 copy.76
  105.6 0.2 broadcast_in_dim.35
  105.8 1.4 copy.85
  107.1 40.9 %reduce-scatter.3.cloned.1.call-done = f32[48,512]{1,0:T(8,128)} async-done(((f32[48,4096]{1,0:T(8,128)}), f32[48,512]{1,0:T(8,128)}) %reduce-scatter.3.cloned.1.call-update) | async-done | bytes 98320 | tf_op jit(solution)/shard_map/reduce_scatter | solution.py:116
  148.0 3.7 fusion.41
  151.8 72.8 %all-reduce.3.cloned.1.call-done = f32[48,3584]{1,0:T(8,128)} async-done(((f32[48,3584]{1,0:T(8,128)}), f32[48,3584]{1,0:T(8,128)}) %all-reduce.3.cloned.1.call-update) | async-done | bytes 688144 | tf_op jit(solution)/shard_map/psum | solution.py:121
  224.7 1.2 multiply_reduce_fusion.2
  226.0 1.6 multiply_reduce_fusion.1
  227.6 0.8 copy-done.1
  228.4 0.1 multiply_convert_fusion
  228.6 0.1 collective-permute-start
  228.6 6.7 %collective-permute-done = bf16[48,3584]{1,0:T(8,128)(2,1)S(1)} collective-permute-done((bf16[48,3584]{1,0:T(8,128)(2,1)S(1)}, bf16[48,3584]{1,0:T(8,128)(2,1)S(1)}, u32[]{:S(2)}, u32[]{:S(2)}) %collective-permute-start) | collective-permute-done | bytes 344096 | tf_op jit(solution)/shard_map/ppermute | solution.py:126
  235.3 6.8 %collective-permute-done.1 = bf16[48,3584]{1,0:T(8,128)(2,1)} collective-permute-done((bf16[48,3584]{1,0:T(8,128)(2,1)S(1)}, bf16[48,3584]{1,0:T(8,128)(2,1)}, u32[]{:S(2)}, u32[]{:S(2)}) %collective-permute-start.1) | collective-permute-done | bytes 344096 | tf_op jit(solution)/shard_map/ppermute | solution.py:126
  242.1 7.0 %collective-permute-done.2 = bf16[48,3584]{1,0:T(8,128)(2,1)} collective-permute-done((bf16[48,3584]{1,0:T(8,128)(2,1)}, bf16[48,3584]{1,0:T(8,128)(2,1)}, u32[]{:S(2)}, u32[]{:S(2)}) %collective-permute-start.2) | collective-permute-done | bytes 344096 | tf_op jit(solution)/shard_map/ppermute | solution.py:126
  249.1 1.0 constant_dynamic-update-slice_fusion.7
  250.1 1.2 constant_dynamic-update-slice_fusion.6
  251.3 1.2 constant_dynamic-update-slice_fusion.4
  252.5 1.0 constant_dynamic-update-slice_fusion.3
  253.5 1.0 constant_dynamic-update-slice_fusion.2
  254.6 0.1 constant_dynamic-update-slice_fusion
  254.7 1.6 copy-done.4
  256.3 1.8 fusion.9
  258.1 6.1 %fusion.31 = f32[192,3584]{1,0:T(8,128)} fusion(bf16[448,3584]{1,0:T(8,128)(2,1)S(1)} %copy-done, f32[192,448]{1,0:T(8,128)} %fusion.9, bf16[3584,448]{0,1:T(8,128)(2,1)} %param.23, bf16[384,3584]{1,0:T(8,128)(2,1)} %copy-done.4, s32[]{:T(128)S(6)} %select_n.32), kind=kOutput, calls=%fused_computation.38 | convolution fusion | flops 1233985536 | bytes 10944516 | tf_op jit(solution)/shard_map/dot_general | solution.py:133
  264.3 34.6 %reduce-scatter.5.cloned.1.call-done = f32[48,3584]{1,0:T(8,128)} async-done(((f32[192,3584]{1,0:T(8,128)}), f32[48,3584]{1,0:T(8,128)}) %reduce-scatter.5.cloned.1.call-update) | async-done | bytes 688144 | tf_op jit(solution)/shard_map/reduce_scatter | solution.py:134
  298.9 77.4 %all-reduce.5.cloned.1.call-done = f32[48,3584]{1,0:T(8,128)} async-done(((f32[48,3584]{1,0:T(8,128)}), f32[48,3584]{1,0:T(8,128)}) %all-reduce.5.cloned.1.call-update) | async-done | bytes 688144 | tf_op jit(solution)/shard_map/psum | solution.py:135
  376.2 1.2 multiply_reduce_fusion
  377.5 1.5 add_convert_fusion
  379.0 0.8 reshape.159
  379.8 2.0 copy.77
  (51 shorter events, 0.3 us)
Async XLA Ops:
  6.5 251.6 %copy-start = (bf16[448,3584]{1,0:T(8,128)(2,1)S(1)}, bf16[448,3584]{1,0:T(8,128)(2,1)}, u32[]{:S(2)}) copy-start(bf16[448,3584]{1,0:T(8,128)(2,1)} %param.25) | copy-start | bytes 9633796
  6.5 5.7 %copy-start.8 = (f32[3584]{0:T(1024)S(1)}, f32[3584]{0:T(1024)}, u32[]{:S(2)}) copy-start(f32[3584]{0:T(1024)} %param.26) | copy-start | bytes 43012
  6.5 141.5 %reduce-scatter.3.cloned.1.call-start = ((), (), s32[]{:S(2)}) async-start(), calls=%async_computation.2 | async-start | bytes 884736 | tf_op jit(solution)/shard_map/reduce_scatter | solution.py:116
  17.0 35.7 %copy-start.14 = (s32[48]{0:T(128)S(1)}, s32[48]{0:T(128)}, u32[]{:S(2)}) copy-start(s32[48]{0:T(128)} %param.19) | copy-start | bytes 580
  17.0 35.8 %copy-start.15 = (s32[48]{0:T(128)S(1)}, s32[48]{0:T(128)}, u32[]{:S(2)}) copy-start(s32[48]{0:T(128)} %param.20) | copy-start | bytes 580
  17.0 36.3 %copy-start.12 = (s32[1,512]{1,0:T(1,128)S(1)}, s32[1,512]{1,0:T(1,128)}, u32[]{:S(2)}) copy-start(s32[1,512]{1,0:T(1,128)} %param.18) | copy-start | bytes 6148
  76.0 2.9 copy-start.3
  76.1 2.9 copy-start.5
  83.8 140.9 %all-reduce.3.cloned.1.call-start = ((), (), s32[]{:S(2)}) async-start(), calls=%async_computation.3 | async-start | bytes 1376256 | tf_op jit(solution)/shard_map/psum | solution.py:121
  148.0 77.9 %copy-start.9 = (f32[3584]{0:T(1024)S(1)}, f32[3584]{0:T(1024)}, u32[]{:S(2)}) copy-start(f32[3584]{0:T(1024)} %param.27) | copy-start | bytes 43012
  151.8 76.7 %copy-start.6 = (f32[3584]{0:T(1024)S(1)}, f32[3584]{0:T(1024)}, u32[]{:S(2)}) copy-start(f32[3584]{0:T(1024)} %param.28) | copy-start | bytes 43012
  151.8 147.1 %reduce-scatter.5.cloned.1.call-start = ((), (), s32[]{:S(2)}) async-start(), calls=%async_computation.4 | async-start | bytes 3440640 | tf_op jit(solution)/shard_map/reduce_scatter | solution.py:134
  227.6 0.9 copy-start.1
  227.6 14.5 %copy-start.10 = (f32[48]{0:T(128)}, f32[48]{0:T(128)S(1)}, u32[]{:S(2)}) copy-start(f32[48]{0:T(128)S(1)} %add_rsqrt_fusion.2) | copy-start | bytes 580
  228.6 6.7 %collective-permute-start = (bf16[48,3584]{1,0:T(8,128)(2,1)S(1)}, bf16[48,3584]{1,0:T(8,128)(2,1)S(1)}, u32[]{:S(2)}, u32[]{:S(2)}) collective-permute-start(bf16[48,3584]{1,0:T(8,128)(2,1)S(1)} %multiply_convert_fusion), channel_id=1, source_target_pairs={{0,8},{8,16},{16,24},{24,0},{1,9},{9,17},{17,25},{25,1},{2,10},{10... | collective-permute-start | bytes 1032200 | tf_op jit(solution)/shard_map/ppermute | solution.py:126
  235.3 6.8 %collective-permute-start.1 = (bf16[48,3584]{1,0:T(8,128)(2,1)S(1)}, bf16[48,3584]{1,0:T(8,128)(2,1)}, u32[]{:S(2)}, u32[]{:S(2)}) collective-permute-start(bf16[48,3584]{1,0:T(8,128)(2,1)S(1)} %collective-permute-done), channel_id=1, source_target_pairs={{0,8},{8,16},{16,24},{24,0},{1,9},{9,17},{17,25},{25,1},{2,10},{10... | collective-permute-start | bytes 1032200 | tf_op jit(solution)/shard_map/ppermute | solution.py:126
  242.1 7.0 %collective-permute-start.2 = (bf16[48,3584]{1,0:T(8,128)(2,1)}, bf16[48,3584]{1,0:T(8,128)(2,1)}, u32[]{:S(2)}, u32[]{:S(2)}) collective-permute-start(bf16[48,3584]{1,0:T(8,128)(2,1)} %collective-permute-done.1), channel_id=1, source_target_pairs={{0,8},{8,16},{16,24},{24,0},{1,9},{9,17},{17,25},{25,1},{2,10},{10... | collective-permute-start | bytes 1032200 | tf_op jit(solution)/shard_map/ppermute | solution.py:126
  242.1 12.5 %copy-start.2 = (f32[48,3584]{1,0:T(8,128)S(1)}, f32[48,3584]{1,0:T(8,128)}, u32[]{:S(2)}) copy-start(f32[48,3584]{1,0:T(8,128)} %copy-done.1) | copy-start | bytes 2064388
  242.1 12.5 %copy-start.7 = (f32[3584]{0:T(1024)S(1)}, f32[3584]{0:T(1024)}, u32[]{:S(2)}) copy-start(f32[3584]{0:T(1024)} %param.28) | copy-start | bytes 43012
  242.1 12.5 %copy-start.11 = (f32[48]{0:T(128)S(1)}, f32[48]{0:T(128)}, u32[]{:S(2)}) copy-start(f32[48]{0:T(128)} %copy-done.10) | copy-start | bytes 580
  250.1 6.2 %copy-start.13 = (bf16[3584,448]{0,1:T(8,128)(2,1)S(1)}, bf16[3584,448]{0,1:T(8,128)(2,1)}, u32[]{:S(2)}) copy-start(bf16[3584,448]{0,1:T(8,128)(2,1)} %param.24) | copy-start | bytes 9633796
  254.7 1.6 copy-start.4
  264.2 112.0 %all-reduce.5.cloned.1.call-start = ((), (), s32[]{:S(2)}) async-start(), calls=%async_computation.5 | async-start | bytes 1376256 | tf_op jit(solution)/shard_map/psum | solution.py:135
Sparse Core Ops, SparseCore 0:
  83.9 64.0 reduce-scatter.2
  151.9 72.7 all-reduce.2
  264.4 34.4 reduce-scatter.4
  302.5 73.6 all-reduce.4
